TPU v7x, 32 devices: a whole 2x2x4 slice. The times are simulated.
32 devices in a mesh: groups: 2 (over x), wide: 4 (over y, core), pair: 4 (over z).
Axes of the slice: x: 2, y: 2, z: 4, core: 2. Of those that a mesh axis runs over, the one named last changes fastest.
Arguments:
- strips: bfloat16 [8, 2, 4096, 256], P(('groups', 'wide'), None, 'pair'), parts along dimension 0, may hold values from -80 to 80
- offsets: int32 [16, 4, 2], P('groups'), parts along dimension 0, may hold values from 0 to 3328, as said below
- block_subgrid: int32 [64], P(('groups', 'wide', 'pair')), parts along dimension 0, may hold values from 0 to 1
- block_kernel: int32 [64, 2], P(('groups', 'wide', 'pair')), parts along dimension 0, may hold values from 0 to 15
- vis_cells: int32 [64, 2, 2048], P(('groups', 'wide', 'pair')), parts along dimension 0, may hold values from 0 to 248
Outputs:
- predicted: float32 [64, 2, 2048], P(('groups', 'wide', 'pair')), parts along dimension 0
There are 2 independent parts, one for each index of `groups`. A program takes and returns all parts, laid end to end along the dimension named above; each array names one. Nothing has to cross between parts.
Inputs may be any that keep to these rules, and one draw needn't show every extreme that they name: offsets[..., 0] lies in 0 to 3328 and offsets[..., 1] in 0 to 255; both ends of both ranges occur.
All inputs are finite; a program needn't handle non-finite values.
Results may differ from a plain program's by a relative error of at most 0.0033.
The roundings to bfloat16 on the way count: a program that leaves them out, or rounds other values in their place, can miss the bound.
Values may be sent and summed in bfloat16 or wider, within the bound.
No kernel may reach another device: no remote copies, remote signals or barrier semaphores. Data moves between devices by JAX's collectives and lax.ppermute only.
A program may use at most 64 MiB of HBM per device.

v0:
```python
import math
import jax
import jax.numpy as jnp
from jax import lax
from jax.sharding import PartitionSpec as P

L = 4096
SUBW = 256
NVIS = 2048
SUPPORT = 8
OVERSAMPLE = 16
SG_WIDE = 2


def strip_block(row_ids, shift, row_index, length):
    frequency = row_ids - SUBW // 2 + shift
    product = frequency[:, None] * row_index[None, :] % length
    phase_arg = 2.0 * math.pi / length * product.astype(jnp.float32)
    centred = (2 * row_index + 1).astype(jnp.float32) / length - 1.0
    taper = (1.0 - 0.5 * centred * centred) / math.sqrt(length)
    cosine = jnp.cos(phase_arg) * taper[None, :]
    sine = jnp.sin(phase_arg) * taper[None, :]
    upper = jnp.concatenate([cosine, sine], axis=1)
    lower = jnp.concatenate([-sine, cosine], axis=1)
    return jnp.concatenate([upper, lower], axis=0).astype(jnp.bfloat16)


def column_ramp(stacked, shift):
    half = stacked.shape[0] // 2
    part_re = stacked[:half]
    part_im = stacked[half:]
    column_ids = jnp.arange(SUBW, dtype=jnp.int32)
    phase_arg = 2.0 * math.pi / SUBW * (shift * column_ids % SUBW).astype(jnp.float32)
    cosine = jnp.cos(phase_arg)[None, :]
    sine = jnp.sin(phase_arg)[None, :]
    out_re = part_re * cosine + part_im * sine
    out_im = part_im * cosine - part_re * sine
    return jnp.concatenate([out_re, out_im], axis=1)


def transform_table():
    grid_ids = jnp.arange(SUBW, dtype=jnp.int32)
    phase_arg = (
        2.0 * math.pi / SUBW * (grid_ids[:, None] * grid_ids[None, :] % SUBW).astype(jnp.float32)
    )
    cosine = jnp.cos(phase_arg) / math.sqrt(SUBW)
    sine = jnp.sin(phase_arg) / math.sqrt(SUBW)
    upper = jnp.concatenate([cosine, -sine], axis=1)
    lower = jnp.concatenate([sine, cosine], axis=1)
    return jnp.concatenate([upper, lower], axis=0).astype(jnp.bfloat16)


def kernel_taps(fraction):
    points = jnp.arange(SUPPORT, dtype=jnp.float32)
    centre = (SUPPORT - 1) / 2.0 + (fraction.astype(jnp.float32) + 0.5) / OVERSAMPLE - 0.5
    distance = points[None, :] - centre[:, None]
    values = jnp.exp(-distance * distance / 2.88)
    return values / jnp.sum(values, axis=-1, keepdims=True)


def column_sum(spread_rows, col_ids, col_taps):
    columns = jnp.arange(SUBW, dtype=jnp.int32)
    distance = columns[None, None, :] - col_ids[:, :, None]
    weights = jnp.zeros(distance.shape, jnp.float32)
    for tap_index in range(SUPPORT):
        weight = col_taps[:, tap_index][:, None, None]
        weights = jnp.where(distance == tap_index, weight, weights)
    real_part = jnp.sum(weights * spread_rows[..., :SUBW], axis=-1)
    imag_part = jnp.sum(weights * spread_rows[..., SUBW:], axis=-1)
    return jnp.stack([real_part, imag_part], axis=-2)


def on_device(strips, offsets, block_subgrid, block_kernel, vis_cells):
    pair_count = lax.axis_size("pair")
    facet_id = lax.axis_index("wide")
    pair_id = lax.axis_index("pair")
    rows_dev = SG_WIDE * SUBW // pair_count
    local_rows = strips.shape[2]
    xstack = strips.reshape(2 * local_rows, SUBW)
    row_index = pair_id * local_rows + jnp.arange(local_rows, dtype=jnp.int32)

    def single(block_no):
        first = block_no * rows_dev
        subgrid_id = first // SUBW
        row_ids = first % SUBW + jnp.arange(rows_dev, dtype=jnp.int32)
        factor = strip_block(row_ids, offsets[subgrid_id, facet_id, 0], row_index, L)
        product = jnp.dot(factor, xstack, preferred_element_type=jnp.float32)
        return column_ramp(product, offsets[subgrid_id, facet_id, 1])

    stacked = lax.map(
        single, jnp.arange(rows_dev * lax.axis_size(("wide", "pair")) // rows_dev, dtype=jnp.int32)
    )
    summed = lax.psum_scatter(
        stacked.reshape(rows_dev * lax.axis_size(("wide", "pair")), 2 * SUBW),
        ("wide", "pair"),
        scatter_dimension=0,
        tiled=True,
    )
    subgrid = summed.astype(jnp.bfloat16)
    spectrum = jnp.dot(subgrid, transform_table(), preferred_element_type=jnp.float32).astype(
        jnp.bfloat16
    )
    blocks = vis_cells.shape[0]
    row_taps = kernel_taps(block_kernel[:, 0]).astype(jnp.bfloat16)
    col_taps = kernel_taps(block_kernel[:, 1])
    row_base = block_subgrid[:, None] * SUBW + vis_cells[:, 0, :]
    portion = lax.all_gather(spectrum, "pair", axis=0, tiled=True)
    amount = portion.shape[0]
    row_ids = jnp.arange(amount, dtype=jnp.int32)
    distance = row_ids[None, None, :] - row_base[:, :, None]
    dense = jnp.zeros(distance.shape, jnp.float32)
    for tap_index in range(SUPPORT):
        weight = row_taps[:, tap_index].astype(jnp.float32)[:, None, None]
        dense = jnp.where(distance == tap_index, weight, dense)
    dense = dense.astype(jnp.bfloat16).reshape(blocks * NVIS, amount)
    gathered = jnp.dot(dense, portion, preferred_element_type=jnp.float32)
    spread = gathered.reshape(blocks, NVIS, 2 * SUBW)
    return column_sum(spread, vis_cells[:, 1, :], col_taps)


def solution(mesh):
    placed = (
        P(("groups", "wide"), None, "pair", None),
        P("groups", None, None),
        P(("groups", "wide", "pair")),
        P(("groups", "wide", "pair"), None),
        P(("groups", "wide", "pair"), None, None),
    )
    return jax.shard_map(
        on_device,
        mesh=mesh,
        in_specs=placed,
        out_specs=P(("groups", "wide", "pair"), None, None),
        check_vma=False,
    )
```

profile of v0, /device:TPU:0, one launch (start us, length us, event | category | flops | bytes accessed | tf_op | source)
XLA Modules:
  0.0 266.4 jit_solution(9362500942435788892)
XLA Ops:
  6.5 151.5 %while.14 = (s32[]{:T(128)}, f32[16,128,512]{2,1,0:T(8,128)}, s32[16]{0:T(128)S(1)}, s32[8,4,2]{0,2,1:T(2,128)}, s32[]{:T(128)}, /*index=5*/bf16[2048,256]{1,0:T...) while((s32[]{:T(128)}, f32[16,128,512]{2,1,0:T(8,128)}, ...), condition=%wide.region_3.4_spmd.clone, body=%wide.region_2.3_spmd.clone.sunk | while | flops 275528608 | bytes 5003174 | solution.py:90
  10.0 2.5 fusion.103
  12.4 1.8 fusion.104
  19.4 2.5 fusion.103
  28.9 2.5 fusion.103
  31.4 1.8 fusion.104
  38.3 2.5 fusion.103
  47.8 2.5 fusion.103
  57.3 2.5 fusion.103
  66.8 2.5 fusion.103
  76.2 2.5 fusion.103
  78.7 1.8 fusion.104
  85.7 2.5 fusion.103
  95.2 2.5 fusion.103
  104.6 2.5 fusion.103
  114.1 2.5 fusion.103
  123.6 2.5 fusion.103
  133.0 2.5 fusion.103
  142.5 2.5 fusion.103
  152.0 2.5 fusion.103
  161.4 72.2 %reduce-scatter.2.cloned.1.call-done = f32[128,512]{1,0:T(8,128)} async-done(((f32[2048,512]{1,0:T(8,128)}), f32[128,512]{1,0:T(8,128)}) %reduce-scatter.2.cloned.1.call-update) | async-done | bytes 262160 | tf_op jit(solution)/shard_map/reduce_scatter | solution.py:93
  234.8 14.9 %all_gather.3 = bf16[512,512]{0,1:T(8,128)(2,1)S(1)} all-gather(bf16[128,512]{0,1:T(8,128)(2,1)S(1)} %convolution_convert_fusion), channel_id=1, replica_groups=mesh['groups'=2,'wide'=4,'pair'=4] {'pair'}, dimensions={0}, use_global_device_ids=true | all-gather | bytes 655360 | tf_op jit(solution)/shard_map/all_gather | solution.py:107
  249.7 6.0 %fusion.30 = f32[2,2048,512]{1,2,0:T(8,128)S(1)} fusion(bf16[2]{0:T(256)(128)(2,1)S(1)} %get-tuple-element.198, bf16[2]{0:T(256)(128)(2,1)S(1)} %get-tuple-element.199, bf16[2]{0:T(256)(128)(2,1)S(1)} %get-tuple-element.200, bf16[2]{0:T(256)(128)(2,1)S(1)} %get-tuple-element.201, bf16[2]{0:T(256)(128)(2,1)S(1)} %get-tuple-element.202, ...), kind=kOutput, calls=%fused_computation.51 | convolution fusion | flops 2183135232 | bytes 8929312 | tf_op jit(solution)/shard_map/dot_general | solution.py:116
  255.7 3.2 %fusion.32 = (f32[2,2048]{1,0:T(2,128)S(1)}, f32[2,2048]{1,0:T(2,128)S(1)}) fusion(f32[2,2048,512]{1,2,0:T(8,128)S(1)} %fusion.30, f32[2]{0:T(128)S(1)} %get-tuple-element.190, f32[2]{0:T(128)S(1)} %get-tuple-element.191, f32[2]{0:T(128)S(1)} %get-tuple-element.192, f32[2]{0:T(128)S(1)} %get-tuple-element.193, f32[2]{0:T(128)S(1)} %get-tuple-element.194, ...), kind=kLoop, calls=%fused_computation.55 | loop fusion | flops 22011904 | bytes 8437824 | tf_op jit(solution)/shard_map/reduce_sum | solution.py:68
  (198 shorter events, 99.2 us)
Async XLA Ops:
  6.5 227.0 %reduce-scatter.2.cloned.1.call-start = ((), (), s32[]{:S(2)}) async-start(), calls=%async_computation.1 | async-start | bytes 4456448 | tf_op jit(solution)/shard_map/reduce_scatter | solution.py:93
  158.0 0.8 copy-start
  158.0 0.8 copy-start.1
  158.0 3.2 %copy-start.2 = (s32[2]{0:T(128)S(1)}, s32[2]{0:T(128)}, u32[]{:S(2)}) copy-start(s32[2]{0:T(128)} %param.9) | copy-start | bytes 28
Sparse Core Ops, SparseCore 0:
  158.2 75.2 reduce-scatter.1
where the time goes:
time: 268 us; the launch traced here: 266 us
  waiting for transfers between devices  72.2 us (27%)
  other arithmetic  69.1 us (26%)
  local copies, waits for them, and re-layouts  48.5 us (18%)
  matrix products  35.7 us (13%)
  blocking collectives  14.9 us (6%)
  between operations  13.5 us (5%)
  loops' own time  12.6 us (5%)
    reduce_scatter x1, waiting for transfers between devices, on_device(): lax.psum_scatter(stacked.reshape(rows_dev * lax.axis_size(('wide', 'pair'...  72.2 us
    another operation x18, other arithmetic  41.8 us
    dot_general x16, matrix products, single(): product = jnp.dot(factor, xstack, preferred_element_type=jnp.float32)  28.4 us
    dynamic_slice x16, local copies, waits for them, and re-layouts, single(): return column_ramp(product, offsets[subgrid_id, facet_id, 1])  22.8 us
    all_gather x1, blocking collectives, on_device(): portion = lax.all_gather(spectrum, 'pair', axis=0, tiled=True)  14.9 us
    dynamic_update_slice x32, local copies, waits for them, and re-layouts, on_device(): lax.map(single, jnp.arange(rows_dev * lax.axis_size(('wide', 'pair')) //...  13.8 us
    another operation x1, loops' own time, on_device(): lax.map(single, jnp.arange(rows_dev * lax.axis_size(('wide', 'pair')) //...  12.6 us
    sin x16, other arithmetic, column_ramp(): sine = jnp.sin(phase_arg)[None, :]  11.8 us
  transfers between devices with their start and end apart: 1, of which 1 were waited for; matrix products, arithmetic and copies ran while one was open for 1% of the time, Pallas kernels for 0%

commit v1 on v0

--- a/solution.py
+++ b/solution.py
@@ -104,7 +104,9 @@
     row_taps = kernel_taps(block_kernel[:, 0]).astype(jnp.bfloat16)
     col_taps = kernel_taps(block_kernel[:, 1])
     row_base = block_subgrid[:, None] * SUBW + vis_cells[:, 0, :]
-    portion = lax.all_gather(spectrum, "pair", axis=0, tiled=True)
+    portion = jnp.concatenate(
+        lax.all_to_all(jnp.stack([spectrum] * lax.axis_size("pair")), "pair", 0, 0), axis=0
+    )
     amount = portion.shape[0]
     row_ids = jnp.arange(amount, dtype=jnp.int32)
     distance = row_ids[None, None, :] - row_base[:, :, None]

time: 268 us -> 271 us (1.011)
  blocking collectives: 14.9 us -> 0 us
  waiting for transfers between devices: 72.2 us -> 85.1 us
  starting transfers between devices: 0.01 us -> 3.47 us
    all_gather x1 -> x0, blocking collectives: 14.9 us -> none  [on_device(): portion = lax.all_gather(spectrum, 'pair', axis=0, tiled=True)]
    all_to_all x0 -> x1, waiting for transfers between devices: none -> 12.9 us  [on_device(): lax.all_to_all(jnp.stack([spectrum] * lax.axis_size('pair')), 'pair', 0, 0)]
    all_to_all x0 -> x1, starting transfers between devices: none -> 3.47 us  [on_device(): lax.all_to_all(jnp.stack([spectrum] * lax.axis_size('pair')), 'pair', 0, 0)]
  transfers between devices with their start and end apart: 1 -> 2, of which waited for: 1 -> 2; matrix products, arithmetic and copies ran while one was open for 1% -> 1% of each run, Pallas kernels for 0% -> 0%
where the time goes in v1:
time: 271 us; the launch traced here: 269 us
  waiting for transfers between devices  85.1 us (31%)
  other arithmetic  69.1 us (25%)
  local copies, waits for them, and re-layouts  50.1 us (18%)
  matrix products  35.6 us (13%)
  between operations  13.5 us (5%)
  loops' own time  12.6 us (5%)
  starting transfers between devices  3.47 us (1%)
    reduce_scatter x1, waiting for transfers between devices, on_device(): lax.psum_scatter(stacked.reshape(rows_dev * lax.axis_size(('wide', 'pair'...  72.3 us
    another operation x18, other arithmetic  41.8 us
    dot_general x16, matrix products, single(): product = jnp.dot(factor, xstack, preferred_element_type=jnp.float32)  28.4 us
    dynamic_slice x16, local copies, waits for them, and re-layouts, single(): return column_ramp(product, offsets[subgrid_id, facet_id, 1])  22.8 us
    dynamic_update_slice x32, local copies, waits for them, and re-layouts, on_device(): lax.map(single, jnp.arange(rows_dev * lax.axis_size(('wide', 'pair')) //...  13.8 us
    all_to_all x1, waiting for transfers between devices, on_device(): lax.all_to_all(jnp.stack([spectrum] * lax.axis_size('pair')), 'pair', 0, 0)  12.9 us
    another operation x1, loops' own time, on_device(): lax.map(single, jnp.arange(rows_dev * lax.axis_size(('wide', 'pair')) //...  12.6 us
    sin x16, other arithmetic, column_ramp(): sine = jnp.sin(phase_arg)[None, :]  11.8 us
  transfers between devices with their start and end apart: 2, of which 2 were waited for; matrix products, arithmetic and copies ran while one was open for 1% of the time, Pallas kernels for 0%

profile of v1, /device:TPU:0, one launch (start us, length us, event | category | flops | bytes accessed | tf_op | source)
XLA Modules:
  0.0 269.5 jit_solution(12594517341160464986)
XLA Ops:
  6.5 151.5 %while.14 = (s32[]{:T(128)}, f32[16,128,512]{2,1,0:T(8,128)}, s32[16]{0:T(128)S(1)}, s32[8,4,2]{0,2,1:T(2,128)}, s32[]{:T(128)}, /*index=5*/bf16[2048,256]{1,0:T...) while((s32[]{:T(128)}, f32[16,128,512]{2,1,0:T(8,128)}, ...), condition=%wide.region_3.4_spmd.clone, body=%wide.region_2.3_spmd.clone.sunk | while | flops 275528608 | bytes 5003174 | solution.py:90
  10.0 2.5 fusion.105
  12.4 1.8 fusion.106
  19.4 2.5 fusion.105
  28.9 2.5 fusion.105
  38.3 2.5 fusion.105
  47.8 2.5 fusion.105
  57.3 2.5 fusion.105
  66.8 2.5 fusion.105
  76.2 2.5 fusion.105
  78.7 1.8 fusion.106
  85.7 2.5 fusion.105
  95.2 2.5 fusion.105
  104.6 2.5 fusion.105
  114.1 2.5 fusion.105
  123.6 2.5 fusion.105
  133.0 2.5 fusion.105
  142.5 2.5 fusion.105
  152.0 2.5 fusion.105
  161.2 72.3 %reduce-scatter.2.cloned.1.call-done = f32[128,512]{1,0:T(8,128)} async-done(((f32[2048,512]{1,0:T(8,128)}), f32[128,512]{1,0:T(8,128)}) %reduce-scatter.2.cloned.1.call-update) | async-done | bytes 262160 | tf_op jit(solution)/shard_map/reduce_scatter | solution.py:93
  235.7 3.5 %all-to-all-start = ((bf16[4,128,512]{1,2,0:T(8,128)(2,1)}), bf16[4,128,512]{1,2,0:T(8,128)(2,1)S(1)}, u32[]{:S(2)}, u32[]{:S(2)}) async-start(bf16[4,128,512]{1,2,0:T(8,128)(2,1)} %stack.16), calls=%async_computation.1 | async-start | bytes 1048576 | tf_op jit(solution)/shard_map/all_to_all | solution.py:108
  239.3 12.9 %all-to-all-done = bf16[4,128,512]{1,2,0:T(8,128)(2,1)S(1)} async-done(((bf16[4,128,512]{1,2,0:T(8,128)(2,1)}), bf16[4,128,512]{1,2,0:T(8,128)(2,1)S(1)}, u32[]{:S(2)}, u32[]{:S(2)}) %all-to-all-start) | async-done | bytes 524320 | tf_op jit(solution)/shard_map/all_to_all | solution.py:108
  252.8 6.0 %fusion.31 = f32[2,2048,512]{1,2,0:T(8,128)S(1)} fusion(bf16[512,512,1]{0,1,2:T(8,128)(2,1)S(1)} %reshape.264, bf16[2]{0:T(256)(128)(2,1)S(1)} %get-tuple-element.198, bf16[2]{0:T(256)(128)(2,1)S(1)} %get-tuple-element.199, bf16[2]{0:T(256)(128)(2,1)S(1)} %get-tuple-element.200, bf16[2]{0:T(256)(128)(2,1)S(1)} %get-tuple-element.201, ...), kind=kOutput, calls=%fused_computation.52 | convolution fusion | flops 2183135232 | bytes 8929312 | tf_op jit(solution)/shard_map/dot_general | solution.py:118
  258.7 3.2 %fusion.34 = (f32[2,2048]{1,0:T(2,128)S(1)}, f32[2,2048]{1,0:T(2,128)S(1)}) fusion(f32[2,2048,512]{1,2,0:T(8,128)S(1)} %fusion.31, f32[2]{0:T(128)S(1)} %get-tuple-element.190, f32[2]{0:T(128)S(1)} %get-tuple-element.191, f32[2]{0:T(128)S(1)} %get-tuple-element.192, f32[2]{0:T(128)S(1)} %get-tuple-element.193, f32[2]{0:T(128)S(1)} %get-tuple-element.194, ...), kind=kLoop, calls=%fused_computation.56 | loop fusion | flops 22011904 | bytes 8437824 | tf_op jit(solution)/shard_map/reduce_sum | solution.py:68
  (203 shorter events, 102.4 us)
Async XLA Ops:
  6.5 227.0 %reduce-scatter.2.cloned.1.call-start = ((), (), s32[]{:S(2)}) async-start(), calls=%async_computation.2 | async-start | bytes 4456448 | tf_op jit(solution)/shard_map/reduce_scatter | solution.py:93
  158.0 0.8 copy-start
  158.0 0.8 copy-start.1
  158.0 81.1 %copy-start.2 = (s32[2]{0:T(128)S(1)}, s32[2]{0:T(128)}, u32[]{:S(2)}) copy-start(s32[2]{0:T(128)} %param.9) | copy-start | bytes 28
  235.7 16.5 %all-to-all-start = ((bf16[4,128,512]{1,2,0:T(8,128)(2,1)}), bf16[4,128,512]{1,2,0:T(8,128)(2,1)S(1)}, u32[]{:S(2)}, u32[]{:S(2)}) async-start(bf16[4,128,512]{1,2,0:T(8,128)(2,1)} %stack.16), calls=%async_computation.1 | async-start | bytes 1048576 | tf_op jit(solution)/shard_map/all_to_all | solution.py:108
Sparse Core Ops, SparseCore 0:
  158.2 75.2 reduce-scatter.1
